TPU v7x, 256 devices: a whole 4x4x8 slice. The times are simulated.
256 devices in a mesh: seq: 16 (over y, z_hi, core), mp: 16 (over z_lo, x).
Axes of the slice: x: 4, y: 4, z: 8 (z_hi: 2, z_lo: 4; z = z_hi * 4 + z_lo), core: 2. Of those that a mesh axis runs over, the one named last changes fastest.
Arguments:
- hidden_in: bfloat16 [2048, 2048], P('seq'), may hold values from -0.59765625 to 0.59765625
- input_gain: float32 [2048], replicated, may hold values from 0.25 to 1.75
- w_query: bfloat16 [2048, 2048], P(None, 'mp'), may hold values from -0.125 to 0.125
- key_value_weight: bfloat16 [2048, 4096], P(None, 'mp'), may hold values from -1 to 1, as said below
- query_gain: float32 [128], replicated, may hold values from 0.25 to 1.75
- key_gain: float32 [128], replicated, may hold values from 0.25 to 1.75
- w_out: bfloat16 [2048, 2048], P('mp'), may hold values from -0.125 to 0.125
- post_gain: float32 [2048], replicated, may hold values from 0.25 to 1.75
- w_gate: bfloat16 [2048, 6144], P(None, 'mp'), may hold values from -0.125 to 0.125
- w_up: bfloat16 [2048, 6144], P(None, 'mp'), may hold values from -0.125 to 0.125
- w_down: bfloat16 [6144, 2048], P('mp'), may hold values from -0.078125 to 0.078125
- prefix_slot_cache: bfloat16 [32, 256, 8, 256], P('seq'), may hold values from -240 to 240, as said below
- block_table: int32 [32], replicated, may hold values from 0 to 31, each once
- request_prefix: int32 [32], replicated, may hold values from 0 to 3
- suffix_lengths: int32 [32], replicated, may hold values from 1 to 256, 2048 in all
Outputs:
- hidden_out: bfloat16 [2048, 2048], P('seq', 'mp')
- suffix_key_values: bfloat16 [2048, 2048], P('seq', 'mp')
Inputs may be any that keep to these rules, and one draw needn't show every extreme that they name: block_table[p * 8 + i] is the slot holding block i of prefix p; every slot appears once. `suffix_lengths`: the lengths add up to 2048 and the longest is exactly 256. `prefix_slot_cache`: per slot, position and key-value head: a key in the first 128 entries, a value in the last 128. `key_value_weight`: columns of key-value head k: 2 equal blocks of 256, starting at k * 2 * 2 * 128.
All inputs are finite; a program needn't handle non-finite values.
Results may differ from a plain program's by a relative error of at most 0.025.
The roundings to bfloat16 on the way count: a program that leaves them out, or rounds other values in their place, can miss the bound.
Values may be sent and summed in bfloat16 or wider, within the bound.
A program may use at most 64 MiB of HBM per device.

v0:
```python
import math
import jax
import jax.numpy as jnp
from jax import lax
from jax.sharding import PartitionSpec as P

QUERY_HEADS = 16
KEY_VALUE_HEADS = 8
HEAD_WIDTH = 128
N_PREFIX = 4
EPSILON = 1e-06
THETA = 1000000.0
NEGATIVE_FLOOR = -1e30


def token_tables(request_prefix, suffix_lengths, positions, prefix_length):
    request_ends = jnp.cumsum(suffix_lengths)
    starts = request_ends - suffix_lengths
    inside = (
        (positions[:, None] >= starts[None, :]) & (positions[:, None] < request_ends[None, :])
    ).astype(jnp.int32)
    request_ids = jnp.arange(suffix_lengths.shape[0], dtype=jnp.int32)
    request_of = jnp.sum(inside * request_ids[None, :], axis=1)
    start_of = jnp.sum(inside * starts[None, :], axis=1)
    prefix_of = jnp.sum(inside * request_prefix[None, :], axis=1)
    rotary_pos = prefix_length + positions - start_of
    return (request_of, prefix_of, rotary_pos)


def row_norm(values, gain):
    return values * lax.rsqrt(jnp.mean(values * values, axis=-1, keepdims=True) + EPSILON) * gain


def head_norm(values, gain):
    return values * lax.rsqrt(jnp.mean(values * values, axis=-1, keepdims=True) + EPSILON) * gain


def rotate(values, rotary_pos):
    half_dim = values.shape[-1] // 2
    freq_ids = jnp.arange(half_dim).astype(jnp.float32)
    inverse = jnp.exp(freq_ids * (-2.0 * math.log(THETA) / values.shape[-1]))
    angles = rotary_pos.astype(jnp.float32)[:, None] * inverse[None, :]
    cosine = jnp.cos(angles)[:, None, :]
    sine_part = jnp.sin(angles)[:, None, :]
    first_half = values[..., :half_dim]
    second_half = values[..., half_dim:]
    return jnp.concatenate(
        [
            first_half * cosine - second_half * sine_part,
            second_half * cosine + first_half * sine_part,
        ],
        axis=-1,
    )


def allowed_keys(query_req, query_pre, query_pos, key_pre, key_req, key_pos):
    same_prefix = key_pre[None, :] == query_pre[:, None]
    same_request = (key_req[None, :] == query_req[:, None]) & (
        key_pos[None, :] <= query_pos[:, None]
    )
    return same_prefix | same_request


def group_partial(query_rows_all, allowed, key_row_block, value_row_block):
    scaling = 1.0 / math.sqrt(query_rows_all.shape[-1])
    scores = (
        jnp.einsum(
            "nkgd,mkd->nkgm", query_rows_all, key_row_block, preferred_element_type=jnp.float32
        )
        * scaling
    )
    allowed_full = allowed[:, None, None, :]
    scores = jnp.where(allowed_full, scores, NEGATIVE_FLOOR)
    highest_score = jnp.max(scores, axis=-1)
    weights = jnp.where(allowed_full, jnp.exp(scores - highest_score[..., None]), 0.0)
    total_weight = jnp.sum(weights, axis=-1)
    rounded = weights.astype(jnp.bfloat16)
    summed = jnp.einsum(
        "nkgm,mkd->nkgd", rounded, value_row_block, preferred_element_type=jnp.float32
    )
    layer_output = (summed / jnp.maximum(total_weight, 1.0)[..., None]).astype(jnp.bfloat16)
    return (highest_score, total_weight, layer_output)


def tile_partials(query_rows, query_req, query_pre, query_pos, bundle, tile_rows):
    key_row_block, value_row_block, key_pre, key_req, key_pos = bundle
    token_count = query_rows.shape[0]
    tile_count = token_count // tile_rows
    shaped = (
        query_rows.reshape((tile_count, tile_rows) + query_rows.shape[1:]),
        query_req.reshape(tile_count, tile_rows),
        query_pre.reshape(tile_count, tile_rows),
        query_pos.reshape(tile_count, tile_rows),
    )

    def one_tile(members):
        tile_queries, tile_req, tile_pre, tile_pos = members
        allowed = allowed_keys(tile_req, tile_pre, tile_pos, key_pre, key_req, key_pos)

        def computed(unused):
            return group_partial(tile_queries, allowed, key_row_block, value_row_block)

        def skipped(unused):
            stats_shape = tile_queries.shape[:-1]
            return (
                jnp.full(stats_shape, NEGATIVE_FLOOR, jnp.float32),
                jnp.zeros(stats_shape, jnp.float32),
                jnp.zeros(tile_queries.shape, jnp.bfloat16),
            )

        return lax.cond(jnp.any(allowed), computed, skipped, 0)

    highest_score, total_weight, layer_output = lax.map(one_tile, shaped)
    stats_shape = (token_count,) + query_rows.shape[1:-1]
    return (
        highest_score.reshape(stats_shape),
        total_weight.reshape(stats_shape),
        layer_output.reshape(query_rows.shape),
    )


def local(
    hidden_in,
    input_gain,
    w_query,
    key_value_weight,
    query_gain,
    key_gain,
    w_out,
    post_gain,
    w_gate,
    w_up,
    w_down,
    prefix_slot_cache,
    block_table,
    request_prefix,
    suffix_lengths,
):
    seq_count = lax.axis_size("seq")
    model_count = lax.axis_size("mp")
    my_seq = lax.axis_index("seq")
    my_model = lax.axis_index("mp")
    rows_here = hidden_in.shape[0]
    local_heads = w_query.shape[1] // HEAD_WIDTH
    group_width = QUERY_HEADS // KEY_VALUE_HEADS
    shared_heads = max(1, local_heads // group_width)
    query_per_head = local_heads // shared_heads
    pair_width = 2 * HEAD_WIDTH
    first_shared = my_model * local_heads // group_width
    blocks_here = prefix_slot_cache.shape[0]
    block_rows = prefix_slot_cache.shape[1]
    cache_extent = blocks_here * block_rows
    slot_total = blocks_here * seq_count
    prefix_length = slot_total // N_PREFIX * block_rows
    all_tokens = rows_here * seq_count
    hidden_f32 = hidden_in.astype(jnp.float32)
    normed = row_norm(hidden_f32, input_gain).astype(jnp.bfloat16)
    own_pos = my_seq * rows_here + jnp.arange(rows_here, dtype=jnp.int32)
    own_req, own_pre, own_rot = token_tables(request_prefix, suffix_lengths, own_pos, prefix_length)
    query_raw = jnp.dot(normed, w_query, preferred_element_type=jnp.float32).reshape(
        rows_here, local_heads, HEAD_WIDTH
    )
    query_rows_all = rotate(head_norm(query_raw, query_gain), own_rot).astype(jnp.bfloat16)
    pair_block = jnp.dot(normed, key_value_weight, preferred_element_type=jnp.float32).astype(
        jnp.bfloat16
    )
    share_ratio = max(1, group_width // local_heads)
    pair_split = pair_block.reshape(rows_here, shared_heads, 2, HEAD_WIDTH)
    key_row_block = rotate(
        head_norm(pair_split[:, :, 0].astype(jnp.float32), key_gain), own_rot
    ).astype(jnp.bfloat16)
    pairs_mine = jnp.stack([key_row_block, pair_split[:, :, 1]], axis=2).reshape(
        rows_here, shared_heads, pair_width
    )
    cache_cols = shared_heads * pair_width // share_ratio
    suffix_key_values = lax.dynamic_slice_in_dim(
        pairs_mine.reshape(rows_here, shared_heads * pair_width),
        my_model % share_ratio * cache_cols,
        cache_cols,
        1,
    )
    slot_ids = jnp.arange(slot_total, dtype=jnp.int32)
    owner_hits = (block_table[:, None] == slot_ids[None, :]).astype(jnp.int32)
    slot_prefix = jnp.sum(owner_hits * (slot_ids // (slot_total // N_PREFIX))[:, None], axis=0)
    cache_mine = lax.dynamic_slice_in_dim(prefix_slot_cache, first_shared, shared_heads, 2).reshape(
        cache_extent, shared_heads, pair_width
    )
    query_all = lax.all_gather(
        query_rows_all.reshape(rows_here, local_heads * HEAD_WIDTH), "seq", axis=0, tiled=True
    )
    query_all = query_all.reshape(all_tokens, shared_heads, query_per_head, HEAD_WIDTH)
    all_pos = jnp.arange(all_tokens, dtype=jnp.int32)
    all_req, all_pre, _ = token_tables(request_prefix, suffix_lengths, all_pos, prefix_length)
    group_pre = jnp.repeat(
        lax.dynamic_slice_in_dim(slot_prefix, my_seq * blocks_here, blocks_here), block_rows
    )
    key_positions = my_seq * rows_here + jnp.arange(rows_here, dtype=jnp.int32)
    group_req, _, _ = token_tables(request_prefix, suffix_lengths, key_positions, prefix_length)
    all_keys = jnp.concatenate([cache_mine[..., :HEAD_WIDTH], pairs_mine[..., :HEAD_WIDTH]], axis=0)
    all_values = jnp.concatenate(
        [cache_mine[..., HEAD_WIDTH:], pairs_mine[..., HEAD_WIDTH:]], axis=0
    )
    key_pre = jnp.concatenate([group_pre, jnp.full((rows_here,), -1, jnp.int32)])
    key_req = jnp.concatenate([jnp.full((cache_extent,), -1, jnp.int32), group_req])
    key_pos = jnp.concatenate([jnp.zeros((cache_extent,), jnp.int32), key_positions])
    bundle = (all_keys, all_values, key_pre, key_req, key_pos)
    highest_score, total_weight, layer_output = tile_partials(
        query_all, all_req, all_pre, all_pos, bundle, min(512, all_tokens)
    )
    highest_score = highest_score.reshape(seq_count, rows_here, shared_heads, query_per_head)
    total_weight = total_weight.reshape(seq_count, rows_here, shared_heads, query_per_head)
    layer_output = layer_output.reshape(
        seq_count, rows_here, shared_heads, query_per_head, HEAD_WIDTH
    )
    widened = lax.optimization_barrier(layer_output).astype(jnp.float32)
    result_back, peak_back, total_back = (
        lax.all_to_all(widened, "seq", split_axis=0, concat_axis=0, tiled=True),
        lax.all_to_all(highest_score, "seq", split_axis=0, concat_axis=0, tiled=True),
        lax.all_to_all(total_weight, "seq", split_axis=0, concat_axis=0, tiled=True),
    )
    best_score = jnp.max(peak_back, axis=0)
    scaling = total_back * jnp.exp(peak_back - best_score[None])
    attended = (
        jnp.sum(scaling[..., None] * result_back, axis=0) / jnp.sum(scaling, axis=0)[..., None]
    )
    attended = attended.astype(jnp.bfloat16).reshape(rows_here, local_heads * HEAD_WIDTH)
    partial_out = jnp.dot(attended, w_out, preferred_element_type=jnp.float32)
    column_count = hidden_in.shape[1] // model_count
    summed = lax.psum(partial_out.astype(jnp.bfloat16), "mp").astype(jnp.float32)
    residual = (hidden_f32 + summed).astype(jnp.bfloat16)
    residual_cols = lax.dynamic_slice_in_dim(residual, my_model * column_count, column_count, 1)
    post_normed = row_norm(residual.astype(jnp.float32), post_gain).astype(jnp.bfloat16)
    gate_terms = jnp.dot(post_normed, w_gate, preferred_element_type=jnp.float32)
    up_terms = jnp.dot(post_normed, w_up, preferred_element_type=jnp.float32)
    middle = (jax.nn.silu(gate_terms) * up_terms).astype(jnp.bfloat16)
    down_terms = jnp.dot(middle, w_down, preferred_element_type=jnp.float32)
    hidden_part = lax.psum_scatter(
        down_terms.astype(jnp.bfloat16), "mp", scatter_dimension=1, tiled=True
    ).astype(jnp.float32)
    hidden_out = (residual_cols.astype(jnp.float32) + hidden_part).astype(jnp.bfloat16)
    return (hidden_out, suffix_key_values)


def solution(mesh):
    in_specs = (
        P("seq", None),
        P(),
        P(None, "mp"),
        P(None, "mp"),
        P(),
        P(),
        P("mp", None),
        P(),
        P(None, "mp"),
        P(None, "mp"),
        P("mp", None),
        P("seq", None, None, None),
        P(),
        P(),
        P(),
    )
    out_specs = (P("seq", "mp"), P("seq", "mp"))
    return jax.shard_map(local, mesh=mesh, in_specs=in_specs, out_specs=out_specs, check_vma=False)
```

profile of v0, /device:TPU:8, one launch (start us, length us, event | category | flops | bytes accessed | tf_op | source)
XLA Modules:
  0.0 402.8 jit_solution(13331135312913714287)
XLA Ops:
  7.3 1.4 fusion.20
  8.7 1.8 convolution_convert_fusion.2
  10.5 0.1 copy.47
  11.1 0.1 reduce.10
  11.4 0.2 select_reduce_fusion
  11.7 0.4 multiply_reduce_fusion.1
  12.3 0.2 fusion.58
  12.6 0.1 copy.59
  12.7 0.1 copy.58
  12.8 33.7 %all_gather.3 = bf16[2048,128]{0,1:T(8,128)(2,1)S(1)} all-gather(bf16[128,128]{0,1:T(8,128)(2,1)S(1)} %pad_maximum_fusion.3), channel_id=1, replica_groups=mesh['seq'=16,'mp'=16] {'seq'}, dimensions={0}, use_global_device_ids=true | all-gather | bytes 557056 | tf_op jit(solution)/shard_map/all_gather | solution.py:188
  46.5 0.3 copy.54
  46.8 0.5 constant_dynamic-slice_fusion.3
  47.5 33.2 %while.14 = (s32[]{:T(128)}, f32[4,512,1,1]{1,3,2,0:T(1,128)S(1)}, f32[4,512,1,1]{1,3,2,0:T(1,128)}, bf16[4,512,1,1,128]{4,1,3,2,0:T(8,128)(2,1)}, s32[640]{0:T(...) while((s32[]{:T(128)}, f32[4,512,1,1]{1,3,2,0:T(1,128)S(1)}, ...), condition=%wide.region_15.16_spmd, body=%wide.region_9.15_spmd.sunk | while | flops 172817920 | bytes 6144739 | solution.py:113
  47.5 1.0 fusion.76
  49.2 4.6 %conditional.2 = (f32[1,512,1,1]{1,3,2,0:T(1,128)}, f32[1,512,1,1]{1,3,2,0:T(1,128)}, bf16[1,512,1,1,128]{4,1,3,2,0:T(8,128)(2,1)S(1)}) conditional(s32[]{:T(128)} %convert_element_type.195, () %tuple.64, (pred[512,640]{1,0:T(32,128)(4,1)S(1)}, bf16[4,512,1,1,128]{4,1,3,2,0:T(8,128)(2,1)S(1)}, s32[]{:T(128)}, bf16[640,1,128]{2,0,1:T(8,128)(2,1)S(1)}, ...), branch_computations={%region_11.11_spmd, %region_12.14_spmd} | conditional | flops 170851840 | bytes 5519388 | solution.py:111
  49.2 1.1 fusion.66
  50.3 1.7 fusion.5
  52.0 0.7 broadcast_maximum_fusion
  52.7 1.1 fusion.3
  53.8 1.3 constant_dynamic-update-slice_fusion.5
  55.1 0.7 constant_dynamic-update-slice_fusion.6
  55.8 1.0 fusion.76
  57.5 4.6 %conditional.2 = (f32[1,512,1,1]{1,3,2,0:T(1,128)}, f32[1,512,1,1]{1,3,2,0:T(1,128)}, bf16[1,512,1,1,128]{4,1,3,2,0:T(8,128)(2,1)S(1)}) conditional(s32[]{:T(128)} %convert_element_type.195, () %tuple.64, (pred[512,640]{1,0:T(32,128)(4,1)S(1)}, bf16[4,512,1,1,128]{4,1,3,2,0:T(8,128)(2,1)S(1)}, s32[]{:T(128)}, bf16[640,1,128]{2,0,1:T(8,128)(2,1)S(1)}, ...), branch_computations={%region_11.11_spmd, %region_12.14_spmd} | conditional | flops 170851840 | bytes 5519388 | solution.py:111
  57.5 1.1 fusion.66
  58.6 1.7 fusion.5
  60.3 0.7 broadcast_maximum_fusion
  61.0 1.1 fusion.3
  62.1 1.3 constant_dynamic-update-slice_fusion.5
  63.4 0.7 constant_dynamic-update-slice_fusion.6
  64.1 1.0 fusion.76
  65.8 4.6 %conditional.2 = (f32[1,512,1,1]{1,3,2,0:T(1,128)}, f32[1,512,1,1]{1,3,2,0:T(1,128)}, bf16[1,512,1,1,128]{4,1,3,2,0:T(8,128)(2,1)S(1)}) conditional(s32[]{:T(128)} %convert_element_type.195, () %tuple.64, (pred[512,640]{1,0:T(32,128)(4,1)S(1)}, bf16[4,512,1,1,128]{4,1,3,2,0:T(8,128)(2,1)S(1)}, s32[]{:T(128)}, bf16[640,1,128]{2,0,1:T(8,128)(2,1)S(1)}, ...), branch_computations={%region_11.11_spmd, %region_12.14_spmd} | conditional | flops 170851840 | bytes 5519388 | solution.py:111
  65.8 1.1 fusion.66
  66.9 1.7 fusion.5
  68.6 0.7 broadcast_maximum_fusion
  69.3 1.1 fusion.3
  70.4 1.3 constant_dynamic-update-slice_fusion.5
  71.7 0.7 constant_dynamic-update-slice_fusion.6
  72.4 1.0 fusion.76
  74.1 4.6 %conditional.2 = (f32[1,512,1,1]{1,3,2,0:T(1,128)}, f32[1,512,1,1]{1,3,2,0:T(1,128)}, bf16[1,512,1,1,128]{4,1,3,2,0:T(8,128)(2,1)S(1)}) conditional(s32[]{:T(128)} %convert_element_type.195, () %tuple.64, (pred[512,640]{1,0:T(32,128)(4,1)S(1)}, bf16[4,512,1,1,128]{4,1,3,2,0:T(8,128)(2,1)S(1)}, s32[]{:T(128)}, bf16[640,1,128]{2,0,1:T(8,128)(2,1)S(1)}, ...), branch_computations={%region_11.11_spmd, %region_12.14_spmd} | conditional | flops 170851840 | bytes 5519388 | solution.py:111
  74.1 1.1 fusion.66
  75.1 1.7 fusion.5
  76.9 0.7 broadcast_maximum_fusion
  77.6 1.1 fusion.3
  78.7 1.3 constant_dynamic-update-slice_fusion.5
  80.0 0.7 constant_dynamic-update-slice_fusion.6
  80.6 13.7 %all_to_all.15 = f32[16,128,1,1]{1,3,2,0:T(1,128)S(1)} all-to-all(f32[16,128,1,1]{1,3,2,0:T(1,128)S(1)} %bitcast.115), channel_id=1, replica_groups=mesh['seq'=16,'mp'=16] {'seq'}, dimensions={0} | all-to-all | bytes 16384 | tf_op jit(solution)/shard_map/all_to_all | solution.py:218
  94.3 4.7 %all-to-all-start = ((f32[16,128,1,1]{1,3,2,0:T(1,128)}), f32[16,128,1,1]{1,3,2,0:T(1,128)S(1)}, u32[]{:S(2)}, u32[]{:S(2)}) async-start(f32[16,128,1,1]{1,3,2,0:T(1,128)} %bitcast.29), calls=%async_computation | async-start | bytes 16384 | tf_op jit(solution)/shard_map/all_to_all | solution.py:219
  99.0 2.1 convert_element_type.121
  101.2 6.5 %all-to-all-done = f32[16,128,1,1]{1,3,2,0:T(1,128)S(1)} async-done(((f32[16,128,1,1]{1,3,2,0:T(1,128)}), f32[16,128,1,1]{1,3,2,0:T(1,128)S(1)}, u32[]{:S(2)}, u32[]{:S(2)}) %all-to-all-start) | async-done | bytes 8224 | tf_op jit(solution)/shard_map/all_to_all | solution.py:219
  107.6 4.9 %all-to-all-start.2 = ((f32[16,128,1,1,128]{4,1,3,2,0:T(8,128)}), f32[16,128,1,1,128]{4,1,3,2,0:T(8,128)S(1)}, u32[]{:S(2)}, u32[]{:S(2)}) async-start(f32[16,128,1,1,128]{4,1,3,2,0:T(8,128)} %convert_element_type.121), calls=%async_computation.2 | async-start | bytes 2097152 | tf_op jit(solution)/shard_map/all_to_all | solution.py:217
  112.6 23.0 %all-to-all-done.2 = f32[16,128,1,1,128]{4,1,3,2,0:T(8,128)S(1)} async-done(((f32[16,128,1,1,128]{4,1,3,2,0:T(8,128)}), f32[16,128,1,1,128]{4,1,3,2,0:T(8,128)S(1)}, u32[]{:S(2)}, u32[]{:S(2)}) %all-to-all-start.2) | async-done | bytes 1048608 | tf_op jit(solution)/shard_map/all_to_all | solution.py:217
  135.6 0.3 multiply_reduce_fusion
  136.0 0.7 copy-done.3
  136.7 1.2 convolution_convert_fusion.1
  137.9 167.1 %all-reduce.5.cloned.1.call-done = bf16[128,2048]{1,0:T(8,128)(2,1)} async-done(((bf16[128,2048]{1,0:T(8,128)(2,1)}), bf16[128,2048]{1,0:T(8,128)(2,1)}) %all-reduce.5.cloned.1.call-update) | async-done | bytes 524304 | tf_op jit(solution)/shard_map/psum | solution.py:229
  305.0 1.4 fusion.17
  306.4 0.1 copy-done.8
  306.6 0.5 fusion.32
  307.0 2.8 convolution_convert_fusion
  309.8 1.0 copy.55
  310.9 0.7 copy.60
  311.6 82.8 %reduce-scatter.4.cloned.1.call-done = bf16[128,128]{1,0:T(8,128)(2,1)} async-done(((bf16[2048,128]{1,0:T(8,128)(2,1)}), bf16[128,128]{1,0:T(8,128)(2,1)}) %reduce-scatter.4.cloned.1.call-update) | async-done | bytes 32784
  394.4 0.9 copy.56
  395.3 0.6 add_convert_fusion
  (78 shorter events, 1.3 us)
Async XLA Ops:
  7.2 39.6 %copy-start = (bf16[2,256,8,256]{3,2,1,0:T(8,128)(2,1)S(1)}, bf16[2,256,8,256]{3,2,1,0:T(8,128)(2,1)}, u32[]{:S(2)}) copy-start(bf16[2,256,8,256]{3,2,1,0:T(8,128)(2,1)} %param.30) | copy-start | bytes 6291460
  7.2 3.5 copy-start.12
  7.3 3.7 copy-start.6
  7.3 4.1 %copy-start.7 = (s32[32]{0:T(128)S(1)}, s32[32]{0:T(128)}, u32[]{:S(2)}) copy-start(s32[32]{0:T(128)} %param.32) | copy-start | bytes 388
  7.3 4.4 %copy-start.1 = (bf16[128,2048]{1,0:T(8,128)(2,1)S(1)}, bf16[128,2048]{1,0:T(8,128)(2,1)}, u32[]{:S(2)}) copy-start(bf16[128,2048]{1,0:T(8,128)(2,1)} %param.19) | copy-start | bytes 1572868
  7.3 4.4 %copy-start.9 = (bf16[2048,128]{1,0:T(8,128)(2,1)S(1)}, bf16[2048,128]{1,0:T(8,128)(2,1)}, u32[]{:S(2)}) copy-start(bf16[2048,128]{1,0:T(8,128)(2,1)} %param.21) | copy-start | bytes 1572868
  7.3 4.4 %copy-start.10 = (f32[2048]{0:T(1024)S(1)}, f32[2048]{0:T(1024)}, u32[]{:S(2)}) copy-start(f32[2048]{0:T(1024)} %param.20) | copy-start | bytes 24580
  10.5 1.6 copy-start.4
  10.5 1.7 copy-start.5
  94.3 13.3 %all-to-all-start = ((f32[16,128,1,1]{1,3,2,0:T(1,128)}), f32[16,128,1,1]{1,3,2,0:T(1,128)S(1)}, u32[]{:S(2)}, u32[]{:S(2)}) async-start(f32[16,128,1,1]{1,3,2,0:T(1,128)} %bitcast.29), calls=%async_computation | async-start | bytes 16384 | tf_op jit(solution)/shard_map/all_to_all | solution.py:219
  107.6 28.0 %all-to-all-start.2 = ((f32[16,128,1,1,128]{4,1,3,2,0:T(8,128)}), f32[16,128,1,1,128]{4,1,3,2,0:T(8,128)S(1)}, u32[]{:S(2)}, u32[]{:S(2)}) async-start(f32[16,128,1,1,128]{4,1,3,2,0:T(8,128)} %convert_element_type.121), calls=%async_computation.2 | async-start | bytes 2097152 | tf_op jit(solution)/shard_map/all_to_all | solution.py:217
  112.5 192.5 %all-reduce.5.cloned.1.call-start = ((), (), s32[]{:S(2)}) async-start(), calls=%async_computation.4 | async-start | bytes 1048576 | tf_op jit(solution)/shard_map/psum | solution.py:229
  135.6 1.0 copy-start.3
  136.0 169.0 %copy-start.2 = (bf16[128,2048]{1,0:T(8,128)(2,1)S(1)}, bf16[128,2048]{1,0:T(8,128)(2,1)}, u32[]{:S(2)}) copy-start(bf16[128,2048]{1,0:T(8,128)(2,1)} %param.19) | copy-start | bytes 1572868
  137.8 168.6 %copy-start.11 = (f32[2048]{0:T(1024)S(1)}, f32[2048]{0:T(1024)}, u32[]{:S(2)}) copy-start(f32[2048]{0:T(1024)} %param.26) | copy-start | bytes 24580
  137.9 256.6 %reduce-scatter.4.cloned.1.call-start = ((), (), s32[]{:S(2)}) async-start(), calls=%async_computation.5 | async-start | bytes 557056
  305.0 1.6 copy-start.8
Sparse Core Ops, SparseCore 0:
  138.0 166.9 all-reduce.4
  311.0 83.4 reduce-scatter.3
where the time goes:
time: 404 us; the launch traced here: 403 us
  waiting for transfers between devices  279 us (69%)
  blocking collectives  47.4 us (12%)
  other arithmetic  20.9 us (5%)
  matrix products  15.3 us (4%)
  between operations  14.5 us (4%)
  local copies, waits for them, and re-layouts  12.8 us (3%)
  starting transfers between devices  9.69 us (2%)
    psum x1, waiting for transfers between devices, local(): lax.psum(partial_out.astype(jnp.bfloat16), 'mp').astype(jnp.float32)  167 us
    unnamed x3, waiting for transfers between devices  82.9 us
    all_gather x1, blocking collectives, local(): lax.all_gather(query_rows_all.reshape(rows_here, local_heads * HEAD_WIDTH...  33.7 us
    all_to_all x1, waiting for transfers between devices, local(): lax.all_to_all(widened, 'seq', split_axis=0, concat_axis=0, tiled=True)  23 us
    all_to_all x1, blocking collectives, local(): lax.all_to_all(highest_score, 'seq', split_axis=0, concat_axis=0, tiled=T...  13.7 us
  transfers between devices with their start and end apart: 4, of which 4 were waited for; matrix products, arithmetic and copies ran while one was open for 1% of the time, Pallas kernels for 0%

commit v1 on v0

--- a/solution.py
+++ b/solution.py
@@ -185,8 +185,16 @@
     cache_mine = lax.dynamic_slice_in_dim(prefix_slot_cache, first_shared, shared_heads, 2).reshape(
         cache_extent, shared_heads, pair_width
     )
-    query_all = lax.all_gather(
-        query_rows_all.reshape(rows_here, local_heads * HEAD_WIDTH), "seq", axis=0, tiled=True
+    query_all = jnp.concatenate(
+        lax.all_to_all(
+            jnp.stack(
+                [query_rows_all.reshape(rows_here, local_heads * HEAD_WIDTH)] * lax.axis_size("seq")
+            ),
+            "seq",
+            0,
+            0,
+        ),
+        axis=0,
     )
     query_all = query_all.reshape(all_tokens, shared_heads, query_per_head, HEAD_WIDTH)
     all_pos = jnp.arange(all_tokens, dtype=jnp.int32)

time: 404 us -> 395 us (0.978)
  blocking collectives: 47.4 us -> 13.8 us
  waiting for transfers between devices: 279 us -> 291 us
  starting transfers between devices: 9.69 us -> 21.3 us
    all_gather x1 -> x0, blocking collectives: 33.7 us -> none  [local(): lax.all_gather(query_rows_all.reshape(rows_here, local_heads * HEAD_WIDTH...]
    all_to_all x0 -> x1, waiting for transfers between devices: none -> 11.7 us  [local(): lax.all_to_all(jnp.stack([query_rows_all.reshape(rows_here, local_heads *...]
    all_to_all x0 -> x1, starting transfers between devices: none -> 11.6 us  [local(): lax.all_to_all(jnp.stack([query_rows_all.reshape(rows_here, local_heads *...]
  transfers between devices with their start and end apart: 4 -> 5, of which waited for: 4 -> 5; matrix products, arithmetic and copies ran while one was open for 1% -> 1% of each run, Pallas kernels for 0% -> 0%
where the time goes in v1:
time: 395 us; the launch traced here: 394 us
  waiting for transfers between devices  291 us (74%)
  other arithmetic  21.6 us (5%)
  starting transfers between devices  21.3 us (5%)
  matrix products  15.4 us (4%)
  between operations  14.5 us (4%)
  local copies, waits for them, and re-layouts  14.2 us (4%)
  blocking collectives  13.8 us (3%)
    psum x1, waiting for transfers between devices, local(): lax.psum(partial_out.astype(jnp.bfloat16), 'mp').astype(jnp.float32)  167 us
    unnamed x3, waiting for transfers between devices  82.9 us
    all_to_all x1, waiting for transfers between devices, local(): lax.all_to_all(widened, 'seq', split_axis=0, concat_axis=0, tiled=True)  22.9 us
    all_to_all x1, blocking collectives, local(): lax.all_to_all(highest_score, 'seq', split_axis=0, concat_axis=0, tiled=T...  13.8 us
    all_to_all x1, waiting for transfers between devices, local(): lax.all_to_all(jnp.stack([query_rows_all.reshape(rows_here, local_heads *...  11.7 us
    all_to_all x1, starting transfers between devices, local(): lax.all_to_all(jnp.stack([query_rows_all.reshape(rows_here, local_heads *...  11.6 us
  transfers between devices with their start and end apart: 5, of which 5 were waited for; matrix products, arithmetic and copies ran while one was open for 1% of the time, Pallas kernels for 0%

profile of v1, /device:TPU:8, one launch (start us, length us, event | category | flops | bytes accessed | tf_op | source)
XLA Modules:
  0.0 394.3 jit_solution(14254599207039932381)
XLA Ops:
  7.2 1.4 fusion.20
  8.6 0.7 copy.48
  9.6 0.7 sub.47
  10.3 1.8 convolution_convert_fusion.2
  12.3 0.4 multiply_reduce_fusion.1
  13.0 0.2 fusion.58
  13.3 0.9 stack.7
  14.2 11.6 %all-to-all-start = ((bf16[16,128,128]{2,1,0:T(8,128)(2,1)}), bf16[16,128,128]{2,1,0:T(8,128)(2,1)S(1)}, u32[]{:S(2)}, u32[]{:S(2)}) async-start(bf16[16,128,128]{2,1,0:T(8,128)(2,1)} %stack.7), calls=%async_computation | async-start | bytes 1048576 | tf_op jit(solution)/shard_map/all_to_all | solution.py:189
  26.0 0.2 select_reduce_fusion
  26.5 0.1 copy.61
  26.7 0.5 constant_dynamic-slice_fusion.3
  27.4 11.7 %all-to-all-done = bf16[16,128,128]{2,1,0:T(8,128)(2,1)S(1)} async-done(((bf16[16,128,128]{2,1,0:T(8,128)(2,1)}), bf16[16,128,128]{2,1,0:T(8,128)(2,1)S(1)}, u32[]{:S(2)}, u32[]{:S(2)}) %all-to-all-start) | async-done | bytes 524320 | tf_op jit(solution)/shard_map/all_to_all | solution.py:189
  39.1 33.2 %while.14 = (s32[]{:T(128)}, f32[4,512,1,1]{1,3,2,0:T(1,128)S(1)}, f32[4,512,1,1]{1,3,2,0:T(1,128)}, bf16[4,512,1,1,128]{4,1,3,2,0:T(8,128)(2,1)}, s32[640]{0:T(...) while((s32[]{:T(128)}, f32[4,512,1,1]{1,3,2,0:T(1,128)S(1)}, ...), condition=%wide.region_15.16_spmd, body=%wide.region_9.15_spmd.sunk | while | flops 172817920 | bytes 6144739 | solution.py:113
  39.1 1.0 fusion.76
  40.8 4.6 %conditional.2 = (f32[1,512,1,1]{1,3,2,0:T(1,128)}, f32[1,512,1,1]{1,3,2,0:T(1,128)}, bf16[1,512,1,1,128]{4,1,3,2,0:T(8,128)(2,1)S(1)}) conditional(s32[]{:T(128)} %convert_element_type.196, () %tuple.63, (pred[512,640]{1,0:T(32,128)(4,1)S(1)}, bf16[4,512,1,1,128]{4,1,3,2,0:T(8,128)(2,1)S(1)}, s32[]{:T(128)}, bf16[640,1,128]{2,0,1:T(8,128)(2,1)S(1)}, ...), branch_computations={%region_11.11_spmd, %region_12.14_spmd} | conditional | flops 170851840 | bytes 5519388 | solution.py:111
  40.9 1.1 fusion.66
  41.9 1.7 fusion.5
  43.7 0.7 broadcast_maximum_fusion
  44.3 1.1 fusion.3
  45.5 1.3 constant_dynamic-update-slice_fusion.5
  46.7 0.7 constant_dynamic-update-slice_fusion.6
  47.4 1.0 fusion.76
  49.1 4.6 %conditional.2 = (f32[1,512,1,1]{1,3,2,0:T(1,128)}, f32[1,512,1,1]{1,3,2,0:T(1,128)}, bf16[1,512,1,1,128]{4,1,3,2,0:T(8,128)(2,1)S(1)}) conditional(s32[]{:T(128)} %convert_element_type.196, () %tuple.63, (pred[512,640]{1,0:T(32,128)(4,1)S(1)}, bf16[4,512,1,1,128]{4,1,3,2,0:T(8,128)(2,1)S(1)}, s32[]{:T(128)}, bf16[640,1,128]{2,0,1:T(8,128)(2,1)S(1)}, ...), branch_computations={%region_11.11_spmd, %region_12.14_spmd} | conditional | flops 170851840 | bytes 5519388 | solution.py:111
  49.2 1.1 fusion.66
  50.2 1.7 fusion.5
  52.0 0.7 broadcast_maximum_fusion
  52.6 1.1 fusion.3
  53.8 1.3 constant_dynamic-update-slice_fusion.5
  55.0 0.7 constant_dynamic-update-slice_fusion.6
  55.7 1.0 fusion.76
  57.4 4.6 %conditional.2 = (f32[1,512,1,1]{1,3,2,0:T(1,128)}, f32[1,512,1,1]{1,3,2,0:T(1,128)}, bf16[1,512,1,1,128]{4,1,3,2,0:T(8,128)(2,1)S(1)}) conditional(s32[]{:T(128)} %convert_element_type.196, () %tuple.63, (pred[512,640]{1,0:T(32,128)(4,1)S(1)}, bf16[4,512,1,1,128]{4,1,3,2,0:T(8,128)(2,1)S(1)}, s32[]{:T(128)}, bf16[640,1,128]{2,0,1:T(8,128)(2,1)S(1)}, ...), branch_computations={%region_11.11_spmd, %region_12.14_spmd} | conditional | flops 170851840 | bytes 5519388 | solution.py:111
  57.5 1.1 fusion.66
  58.5 1.7 fusion.5
  60.3 0.7 broadcast_maximum_fusion
  60.9 1.1 fusion.3
  62.1 1.3 constant_dynamic-update-slice_fusion.5
  63.4 0.7 constant_dynamic-update-slice_fusion.6
  64.0 1.0 fusion.76
  65.7 4.6 %conditional.2 = (f32[1,512,1,1]{1,3,2,0:T(1,128)}, f32[1,512,1,1]{1,3,2,0:T(1,128)}, bf16[1,512,1,1,128]{4,1,3,2,0:T(8,128)(2,1)S(1)}) conditional(s32[]{:T(128)} %convert_element_type.196, () %tuple.63, (pred[512,640]{1,0:T(32,128)(4,1)S(1)}, bf16[4,512,1,1,128]{4,1,3,2,0:T(8,128)(2,1)S(1)}, s32[]{:T(128)}, bf16[640,1,128]{2,0,1:T(8,128)(2,1)S(1)}, ...), branch_computations={%region_11.11_spmd, %region_12.14_spmd} | conditional | flops 170851840 | bytes 5519388 | solution.py:111
  65.8 1.1 fusion.66
  66.8 1.7 fusion.5
  68.6 0.7 broadcast_maximum_fusion
  69.2 1.1 fusion.3
  70.4 1.3 constant_dynamic-update-slice_fusion.5
  71.7 0.7 constant_dynamic-update-slice_fusion.6
  72.3 13.8 %all_to_all.20 = f32[16,128,1,1]{1,3,2,0:T(1,128)S(1)} all-to-all(f32[16,128,1,1]{1,3,2,0:T(1,128)S(1)} %bitcast.117), channel_id=1, replica_groups=mesh['seq'=16,'mp'=16] {'seq'}, dimensions={0} | all-to-all | bytes 16384 | tf_op jit(solution)/shard_map/all_to_all | solution.py:226
  86.2 4.7 %all-to-all-start.1 = ((f32[16,128,1,1]{1,3,2,0:T(1,128)}), f32[16,128,1,1]{1,3,2,0:T(1,128)S(1)}, u32[]{:S(2)}, u32[]{:S(2)}) async-start(f32[16,128,1,1]{1,3,2,0:T(1,128)} %bitcast.30), calls=%async_computation.1 | async-start | bytes 16384 | tf_op jit(solution)/shard_map/all_to_all | solution.py:227
  90.9 2.1 convert_element_type.122
  93.0 6.5 %all-to-all-done.1 = f32[16,128,1,1]{1,3,2,0:T(1,128)S(1)} async-done(((f32[16,128,1,1]{1,3,2,0:T(1,128)}), f32[16,128,1,1]{1,3,2,0:T(1,128)S(1)}, u32[]{:S(2)}, u32[]{:S(2)}) %all-to-all-start.1) | async-done | bytes 8224 | tf_op jit(solution)/shard_map/all_to_all | solution.py:227
  99.5 4.9 %all-to-all-start.3 = ((f32[16,128,1,1,128]{4,1,3,2,0:T(8,128)}), f32[16,128,1,1,128]{4,1,3,2,0:T(8,128)S(1)}, u32[]{:S(2)}, u32[]{:S(2)}) async-start(f32[16,128,1,1,128]{4,1,3,2,0:T(8,128)} %convert_element_type.122), calls=%async_computation.3 | async-start | bytes 2097152 | tf_op jit(solution)/shard_map/all_to_all | solution.py:225
  104.5 22.9 %all-to-all-done.3 = f32[16,128,1,1,128]{4,1,3,2,0:T(8,128)S(1)} async-done(((f32[16,128,1,1,128]{4,1,3,2,0:T(8,128)}), f32[16,128,1,1,128]{4,1,3,2,0:T(8,128)S(1)}, u32[]{:S(2)}, u32[]{:S(2)}) %all-to-all-start.3) | async-done | bytes 1048608 | tf_op jit(solution)/shard_map/all_to_all | solution.py:225
  127.4 0.3 multiply_reduce_fusion
  127.8 0.7 copy-done.3
  128.5 1.2 convolution_convert_fusion.1
  129.7 166.8 %all-reduce.5.cloned.1.call-done = bf16[128,2048]{1,0:T(8,128)(2,1)} async-done(((bf16[128,2048]{1,0:T(8,128)(2,1)}), bf16[128,2048]{1,0:T(8,128)(2,1)}) %all-reduce.5.cloned.1.call-update) | async-done | bytes 524304 | tf_op jit(solution)/shard_map/psum | solution.py:237
  296.5 1.4 fusion.17
  298.0 0.1 copy-done.7
  298.1 0.5 fusion.32
  298.6 2.8 convolution_convert_fusion
  301.4 1.0 copy.58
  302.4 0.7 copy.63
  303.1 82.8 %reduce-scatter.4.cloned.1.call-done = bf16[128,128]{1,0:T(8,128)(2,1)} async-done(((bf16[2048,128]{1,0:T(8,128)(2,1)}), bf16[128,128]{1,0:T(8,128)(2,1)}) %reduce-scatter.4.cloned.1.call-update) | async-done | bytes 32784
  386.0 0.9 copy.59
  386.9 0.6 add_convert_fusion
  (78 shorter events, 1.6 us)
Async XLA Ops:
  7.2 19.5 %copy-start = (bf16[2,256,8,256]{3,2,1,0:T(8,128)(2,1)S(1)}, bf16[2,256,8,256]{3,2,1,0:T(8,128)(2,1)}, u32[]{:S(2)}) copy-start(bf16[2,256,8,256]{3,2,1,0:T(8,128)(2,1)} %param.30) | copy-start | bytes 6291460
  7.2 5.1 %copy-start.1 = (bf16[128,2048]{1,0:T(8,128)(2,1)S(1)}, bf16[128,2048]{1,0:T(8,128)(2,1)}, u32[]{:S(2)}) copy-start(bf16[128,2048]{1,0:T(8,128)(2,1)} %param.19) | copy-start | bytes 1572868
  7.2 5.1 %copy-start.8 = (bf16[2048,128]{1,0:T(8,128)(2,1)S(1)}, bf16[2048,128]{1,0:T(8,128)(2,1)}, u32[]{:S(2)}) copy-start(bf16[2048,128]{1,0:T(8,128)(2,1)} %param.21) | copy-start | bytes 1572868
  7.2 5.1 %copy-start.9 = (f32[2048]{0:T(1024)S(1)}, f32[2048]{0:T(1024)}, u32[]{:S(2)}) copy-start(f32[2048]{0:T(1024)} %param.20) | copy-start | bytes 24580
  10.3 2.4 copy-start.4
  10.3 2.5 copy-start.5
  12.7 13.0 %copy-start.11 = (s32[32]{0:T(128)S(1)}, s32[32]{0:T(128)}, u32[]{:S(2)}) copy-start(s32[32]{0:T(128)} %param.31) | copy-start | bytes 388
  12.7 13.3 %copy-start.6 = (s32[32]{0:T(128)S(1)}, s32[32]{0:T(128)}, u32[]{:S(2)}) copy-start(s32[32]{0:T(128)} %param.32) | copy-start | bytes 388
  14.2 24.9 %all-to-all-start = ((bf16[16,128,128]{2,1,0:T(8,128)(2,1)}), bf16[16,128,128]{2,1,0:T(8,128)(2,1)S(1)}, u32[]{:S(2)}, u32[]{:S(2)}) async-start(bf16[16,128,128]{2,1,0:T(8,128)(2,1)} %stack.7), calls=%async_computation | async-start | bytes 1048576 | tf_op jit(solution)/shard_map/all_to_all | solution.py:189
  86.2 13.3 %all-to-all-start.1 = ((f32[16,128,1,1]{1,3,2,0:T(1,128)}), f32[16,128,1,1]{1,3,2,0:T(1,128)S(1)}, u32[]{:S(2)}, u32[]{:S(2)}) async-start(f32[16,128,1,1]{1,3,2,0:T(1,128)} %bitcast.30), calls=%async_computation.1 | async-start | bytes 16384 | tf_op jit(solution)/shard_map/all_to_all | solution.py:227
  99.5 27.9 %all-to-all-start.3 = ((f32[16,128,1,1,128]{4,1,3,2,0:T(8,128)}), f32[16,128,1,1,128]{4,1,3,2,0:T(8,128)S(1)}, u32[]{:S(2)}, u32[]{:S(2)}) async-start(f32[16,128,1,1,128]{4,1,3,2,0:T(8,128)} %convert_element_type.122), calls=%async_computation.3 | async-start | bytes 2097152 | tf_op jit(solution)/shard_map/all_to_all | solution.py:225
  104.4 192.1 %all-reduce.5.cloned.1.call-start = ((), (), s32[]{:S(2)}) async-start(), calls=%async_computation.5 | async-start | bytes 1048576 | tf_op jit(solution)/shard_map/psum | solution.py:237
  127.4 1.0 copy-start.3
  127.8 168.8 %copy-start.2 = (bf16[128,2048]{1,0:T(8,128)(2,1)S(1)}, bf16[128,2048]{1,0:T(8,128)(2,1)}, u32[]{:S(2)}) copy-start(bf16[128,2048]{1,0:T(8,128)(2,1)} %param.19) | copy-start | bytes 1572868
  129.6 168.3 %copy-start.10 = (f32[2048]{0:T(1024)S(1)}, f32[2048]{0:T(1024)}, u32[]{:S(2)}) copy-start(f32[2048]{0:T(1024)} %param.26) | copy-start | bytes 24580
  129.7 256.3 %reduce-scatter.4.cloned.1.call-start = ((), (), s32[]{:S(2)}) async-start(), calls=%async_computation.6 | async-start | bytes 557056
  296.5 1.6 copy-start.7
Sparse Core Ops, SparseCore 0:
  129.8 166.6 all-reduce.4
  302.5 83.4 reduce-scatter.3
